TPU v7x, 128 devices: a whole 4x4x4 slice. The times are simulated.
128 devices in a mesh: row: 8 (over x, z_hi), col: 16 (over z_lo, y, core).
Axes of the slice: x: 4, y: 4, z: 4 (z_hi: 2, z_lo: 2; z = z_hi * 2 + z_lo), core: 2. Of those that a mesh axis runs over, the one named last changes fastest.
Arguments:
- pair_state: bfloat16 [768, 768, 128], P(('row', 'col')), may hold values from -6 to 6
- single_rep: bfloat16 [16, 768, 768], P(None, ('row', 'col')), may hold values from -64 to 64
- token_mask: int32 [768], replicated, may hold values 0 or 1
- chain_ids: int32 [768], replicated, may hold values from 0 to 3, never falling along the last dimension, each value on 1 to 384 neighbouring positions
- pair_gain: float32 [128], replicated, may hold values from 0.1 to 1.9
- mix_gain: float32 [128], replicated, may hold values from 0.1 to 1.9
- left_weight: bfloat16 [128, 256], replicated, may hold values from -0.5 to 0.5
- right_weight: bfloat16 [128, 256], replicated, may hold values from -0.5 to 0.5
- gate_weight: bfloat16 [128, 128], replicated, may hold values from -0.5 to 0.5
- out_weight: bfloat16 [128, 128], replicated, may hold values from -0.5 to 0.5
- bias_weight: bfloat16 [128, 16], replicated, may hold values from -1.5 to 1.5
- token_weight: bfloat16 [768, 2304], replicated, may hold values from -0.21875 to 0.21875
- merge_weight: bfloat16 [768, 768], replicated, may hold values from -0.625 to 0.625
Outputs:
- pair_tiles: bfloat16 [768, 8, 16, 6, 128], P('row', None, 'col')
- attention_out: bfloat16 [16, 768, 768], P(None, ('row', 'col'))
Inputs may be any that keep to these rules, and one draw needn't show every extreme that they name: chain_ids never falls along the tokens; a chain holds 1 to 384 tokens.
All inputs are finite; a program needn't handle non-finite values.
Results may differ from a plain program's by a relative error of at most 0.034.
Values may be sent and summed in bfloat16 or wider, within the bound.
A program may use at most 256 MiB of HBM per device.

v0:
```python
import math
import jax
import jax.numpy as jnp
from jax import lax
from jax.sharding import PartitionSpec as P

epsilon = 1e-05


def normalize(values, norm_gain):
    floats = values.astype(jnp.float32)
    centered = floats - jnp.mean(floats, axis=-1, keepdims=True)
    variance = jnp.mean(centered * centered, axis=-1, keepdims=True)
    scaled = centered * lax.rsqrt(variance + epsilon)
    if norm_gain is None:
        return scaled
    return scaled * norm_gain


def gated_branch(normed, weight, pair_mask):
    half_width = weight.shape[0]
    hidden = jnp.einsum("ikc,ce->ike", normed, weight, preferred_element_type=jnp.float32)
    return (
        jax.nn.sigmoid(hidden[..., :half_width]) * hidden[..., half_width:] * pair_mask[..., None]
    ).astype(jnp.bfloat16)


def rows_blocks(pair_rows, valid_rows, valid_all, pair_gain, left_weight, group_count, group_rows):
    token_count = pair_rows.shape[1]
    channels = pair_rows.shape[2]

    def one_group(inputs):
        pair_group, valid_group = inputs
        normed_group = normalize(pair_group, pair_gain).astype(jnp.bfloat16)
        left_group = gated_branch(
            normed_group, left_weight, valid_group[:, None] * valid_all[None, :]
        )
        return (normed_group, left_group)

    grouped = (
        pair_rows.reshape(group_count, group_rows, token_count, channels),
        valid_rows.reshape(group_count, group_rows),
    )
    normed_groups, left_groups = lax.map(one_group, grouped)
    return (
        normed_groups.reshape(group_count * group_rows, token_count, channels),
        left_groups.reshape(group_count * group_rows, token_count, channels),
    )


def shards(
    pair_state,
    single_rep,
    token_mask,
    chain_ids,
    pair_gain,
    mix_gain,
    left_weight,
    right_weight,
    gate_weight,
    out_weight,
    bias_weight,
    token_weight,
    merge_weight,
):
    row_count = lax.axis_size("row")
    col_count = lax.axis_size("col")
    row_index = lax.axis_index("row")
    col_index = lax.axis_index("col")
    flat_rows = pair_state.shape[0]
    channels = pair_state.shape[2]
    samples = single_rep.shape[0]
    model_width = single_rep.shape[2]
    head_count = bias_weight.shape[1]
    head_width = model_width // head_count
    block_rows = flat_rows * col_count
    block_cols = flat_rows * row_count
    valid_all = (token_mask == 1).astype(jnp.float32)
    own_start = (row_index * col_count + col_index) * flat_rows
    row_start = row_index * block_rows
    valid_own = lax.dynamic_slice_in_dim(valid_all, own_start, flat_rows)
    valid_rows = lax.dynamic_slice_in_dim(valid_all, row_start, block_rows)
    valid_cols = lax.dynamic_index_in_dim(
        valid_all.reshape(row_count, col_count, flat_rows), col_index, 1, False
    ).reshape(block_cols)
    chain_rows = lax.dynamic_slice_in_dim(chain_ids, row_start, block_rows)
    chain_cols = lax.dynamic_index_in_dim(
        chain_ids.reshape(row_count, col_count, flat_rows), col_index, 1, False
    ).reshape(block_cols)
    projected = jnp.einsum(
        "std,de->ste", single_rep, token_weight, preferred_element_type=jnp.float32
    ).astype(jnp.bfloat16)
    queries = projected[..., :model_width]
    keys_own = projected[..., model_width : 2 * model_width]
    values_own = projected[..., 2 * model_width :]
    normed_own = normalize(pair_state, pair_gain).astype(jnp.bfloat16)
    own_mask = valid_own[:, None] * valid_all[None, :]
    right_own = gated_branch(normed_own, right_weight, own_mask)
    right_cols, keys_cols, values_cols = (
        lax.all_gather(right_own, "row", axis=0, tiled=True),
        lax.all_gather(keys_own, "row", axis=1, tiled=True),
        lax.all_gather(values_own, "row", axis=1, tiled=True),
    )
    pair_rows, query_rows = (
        lax.all_gather(pair_state, "col", axis=0, tiled=True),
        lax.all_gather(queries, "col", axis=1, tiled=True),
    )
    normed_rows, left_rows = rows_blocks(
        pair_rows, valid_rows, valid_all, pair_gain, left_weight, col_count, flat_rows
    )
    pair_tile = lax.dynamic_index_in_dim(
        pair_rows.reshape(block_rows, row_count, col_count, flat_rows, channels),
        col_index,
        2,
        False,
    ).reshape(block_rows, block_cols, channels)
    normed_tile = lax.dynamic_index_in_dim(
        normed_rows.reshape(block_rows, row_count, col_count, flat_rows, channels),
        col_index,
        2,
        False,
    ).reshape(block_rows, block_cols, channels)
    mixed_pairs = jnp.einsum(
        "ikc,jkc->ijc", left_rows, right_cols, preferred_element_type=jnp.float32
    )
    mixed_norm = normalize(mixed_pairs, mix_gain).astype(jnp.bfloat16)
    gate_value = jax.nn.sigmoid(
        jnp.einsum("ijc,ce->ije", normed_tile, gate_weight, preferred_element_type=jnp.float32)
    )
    update = jnp.einsum("ijc,ce->ije", mixed_norm, out_weight, preferred_element_type=jnp.float32)
    pair_new = (pair_tile.astype(jnp.float32) + gate_value * update).astype(jnp.bfloat16)
    bias_input = normalize(pair_new, None).astype(jnp.bfloat16)
    pair_bias = jnp.einsum(
        "ijc,ch->hij", bias_input, bias_weight, preferred_element_type=jnp.float32
    )
    query_heads = query_rows.reshape(samples, block_rows, head_count, head_width)
    key_heads = keys_cols.reshape(samples, block_cols, head_count, head_width)
    value_heads = values_cols.reshape(samples, block_cols, head_count, head_width)
    score_scale = 1.0 / math.sqrt(head_width)
    scores = (
        jnp.einsum("sihd,sjhd->shij", query_heads, key_heads, preferred_element_type=jnp.float32)
        * score_scale
        + pair_bias[None]
    )
    row_ids = row_start + jnp.arange(block_rows, dtype=jnp.int32)
    col_ids = (
        (jnp.arange(row_count, dtype=jnp.int32)[:, None] * col_count + col_index) * flat_rows
        + jnp.arange(flat_rows, dtype=jnp.int32)[None, :]
    ).reshape(block_cols)
    allowed = (valid_cols[None, :] > 0.5) & (chain_rows[:, None] == chain_cols[None, :]) | (
        row_ids[:, None] == col_ids[None, :]
    )
    local_max = jnp.max(jnp.where(allowed[None, None], scores, -1e30), axis=-1)
    row_max = lax.pmax(local_max.astype(jnp.bfloat16), "col").astype(local_max.dtype)
    weights = jnp.where(allowed[None, None], jnp.exp(scores - row_max[..., None]), 0.0).astype(
        jnp.bfloat16
    )
    totals = jnp.sum(weights.astype(jnp.float32), axis=-1)
    summed = jnp.einsum(
        "shij,sjhd->sihd", weights, value_heads, preferred_element_type=jnp.float32
    ).reshape(samples, block_rows, model_width)
    summed_own, totals_own = (
        lax.psum_scatter(
            summed.astype(jnp.bfloat16), "col", scatter_dimension=1, tiled=True
        ).astype(jnp.float32),
        lax.psum_scatter(
            totals.astype(jnp.bfloat16), "col", scatter_dimension=2, tiled=True
        ).astype(jnp.float32),
    )
    attended = (
        summed_own.reshape(samples, flat_rows, head_count, head_width)
        / jnp.transpose(totals_own, (0, 2, 1))[..., None]
    ).astype(jnp.bfloat16)
    attended = attended.reshape(samples, flat_rows, model_width)
    attention_out = jnp.einsum(
        "std,de->ste", attended, merge_weight, preferred_element_type=jnp.float32
    ).astype(jnp.bfloat16)
    return (pair_new.reshape(block_rows, row_count, 1, flat_rows, channels), attention_out)


def solution(mesh):
    in_specs = (
        P(("row", "col"), None, None),
        P(None, ("row", "col"), None),
        P(),
        P(),
        P(),
        P(),
        P(),
        P(),
        P(),
        P(),
        P(),
        P(),
        P(),
    )
    out_specs = (P("row", None, "col", None, None), P(None, ("row", "col"), None))
    return jax.shard_map(shards, mesh=mesh, in_specs=in_specs, out_specs=out_specs, check_vma=False)
```

profile of v0, /device:TPU:0, one launch (start us, length us, event | category | flops | bytes accessed | tf_op | source)
XLA Modules:
  0.0 886.4 jit_solution(9428254966866073664)
XLA Ops:
  21.4 41.2 %all-gather.14.cloned.1.call-done = bf16[16,48,768]{2,0,1:T(8,128)(2,1)} async-done(((bf16[16,6,768]{2,0,1:T(8,128)(2,1)}), bf16[16,48,768]{2,0,1:T(8,128)(2,1)}) %all-gather.14.cloned.1.call-update) | async-done | bytes 1179664 | tf_op jit(solution)/shard_map/all_gather | solution.py:101
  62.6 5.7 reshape.290
  68.4 44.2 %all-gather.10.cloned.1.call-done = bf16[16,48,768]{2,0,1:T(8,128)(2,1)} async-done(((bf16[16,6,768]{2,0,1:T(8,128)(2,1)}), bf16[16,48,768]{2,0,1:T(8,128)(2,1)}) %all-gather.10.cloned.1.call-update) | async-done | bytes 1179664 | tf_op jit(solution)/shard_map/all_gather | solution.py:102
  112.6 4.2 copy.104
  116.8 30.6 %all-gather.12.cloned.1.call-done = bf16[16,96,768]{2,0,1:T(8,128)(2,1)} async-done(((bf16[16,6,768]{2,0,1:T(8,128)(2,1)}), bf16[16,96,768]{2,0,1:T(8,128)(2,1)}) %all-gather.12.cloned.1.call-update) | async-done | bytes 2359312 | tf_op jit(solution)/shard_map/all_gather | solution.py:106
  147.4 4.6 copy.105
  152.0 116.8 %all-gather.8.cloned.1.call-done = bf16[48,768,128]{2,1,0:T(8,128)(2,1)} async-done(((bf16[6,768,128]{2,1,0:T(8,128)(2,1)}), bf16[48,768,128]{2,1,0:T(8,128)(2,1)}) %all-gather.8.cloned.1.call-update) | async-done | bytes 9437200 | tf_op jit(solution)/shard_map/all_gather | solution.py:100
  268.8 13.2 %copy.99 = bf16[48,768,128]{1,0,2:T(8,128)(2,1)} copy(bf16[48,768,128]{2,1,0:T(8,128)(2,1)} %all-gather.8.cloned.1.call-done) | data formatting | bytes 18874368 | tf_op jit(solution)/shard_map/all_gather | solution.py:100
  281.9 87.7 %all-gather.6.cloned.1.call-done = bf16[96,768,128]{2,1,0:T(8,128)(2,1)} async-done(((bf16[6,768,128]{2,1,0:T(8,128)(2,1)}), bf16[96,768,128]{2,1,0:T(8,128)(2,1)}) %all-gather.6.cloned.1.call-update) | async-done | bytes 18874384 | tf_op jit(solution)/shard_map/all_gather | solution.py:105
  369.6 212.1 %while.12 = (s32[]{:T(128)}, bf16[16,6,768,128]{3,2,1,0:T(8,128)(2,1)}, bf16[16,6,768,128]{3,2,1,0:T(8,128)(2,1)}, bf16[16,6,768,128]{3,2,1,0:T(8,128)(2,1)}, f3...) while((s32[]{:T(128)}, ...), condition=%wide.region_3.4_spmd, body=%wide.region_0.0_spmd.sunk | while | flops 314975232 | bytes 16826032 | solution.py:44
  379.1 3.9 fusion.82
  418.9 3.9 fusion.82
  577.9 3.9 fusion.82
  581.7 24.4 %copy.100 = bf16[96,768,128]{1,0,2:T(8,128)(2,1)} copy(bf16[96,768,128]{2,1,0:T(8,128)(2,1)} %bitcast.97) | data formatting | bytes 37748736 | tf_op jit(solution)/shard_map/reshape | solution.py:47
  606.2 12.4 %bitcast_reduce_fusion = (f32[96,48]{0,1:T(8,128)S(1)}, f32[128,48,96]{2,1,0:T(8,128)S(1)}) fusion(bf16[48,768,128]{1,0,2:T(8,128)(2,1)} %copy.99, bf16[96,768,128]{1,0,2:T(8,128)(2,1)} %copy.100), kind=kOutput, calls=%fused_computation.42 | convolution fusion | flops 906554880 | bytes 30689280 | tf_op jit(solution)/shard_map/ikc,jkc->ijc/dot_general | solution.py:123
  624.0 31.1 %reshape_reshape.3 = bf16[96,8,16,6,128]{4,3,2,1,0:T(8,128)(2,1)} reshape(bf16[16,6,768,128]{3,2,1,0:T(8,128)(2,1)} %get-tuple-element.45) | data formatting | bytes 37748736 | tf_op jit(solution)/shard_map/reshape;reshape | solution.py:118
  657.5 16.7 %copy.96 = bf16[96,768,128]{2,0,1:T(8,128)(2,1)S(1)} copy(bf16[96,768,128]{2,1,0:T(8,128)(2,1)} %bitcast.95) | data formatting | bytes 37748736 | tf_op jit(solution)/shard_map/all_gather | solution.py:105
  682.4 9.0 %select_reduce_fusion = (bf16[16,16,96]{2,1,0:T(8,128)(2,1)S(1)}, f32[16,16,96,48]{2,3,1,0:T(8,128)}) fusion(f32[16,96,48]{1,2,0:T(8,128)S(1)} %copy.112, pred[96,48]{0,1:T(8,128)(4,1)S(1)} %compare_or_fusion, bf16[16,96,16,48]{1,3,2,0:T(8,128)(2,1)} %bitcast.101, bf16[16,48,16,48]{3,2,0,1:T(8,128)(2,1)} %reshape.290), kind=kOutput, calls=%fused_computation.34 | convolution fusion | flops 117940224 | bytes 8606208 | tf_op jit(solution)/shard_map/sihd,sjhd->shij/dot_general | solution.py:141
  691.4 55.5 %pmax.7 = bf16[16,16,96]{2,1,0:T(8,128)(2,1)S(1)} all-reduce(bf16[16,16,96]{2,1,0:T(8,128)(2,1)S(1)} %get-tuple-element.90), channel_id=1, replica_groups=mesh['row'=8,'col'=16] {'col'}, use_global_device_ids=true, to_apply=%region_11.12 | all-reduce | flops 24576 | bytes 98304 | tf_op jit(solution)/shard_map/pmax | solution.py:154
  746.9 5.0 fusion.65
  753.3 7.2 convolution_convert_fusion
  760.5 4.9 copy.113
  767.5 44.7 %reduce-scatter.5.cloned.1.call-done = bf16[16,16,6]{1,0,2:T(8,128)(2,1)} async-done(((bf16[16,16,96]{1,0,2:T(8,128)(2,1)}), bf16[16,16,6]{1,0,2:T(8,128)(2,1)}) %reduce-scatter.5.cloned.1.call-update) | async-done | bytes 3088 | tf_op jit(solution)/shard_map/reduce_scatter | solution.py:166
  816.3 60.8 %reduce-scatter.3.cloned.1.call-done = bf16[16,6,768]{2,0,1:T(8,128)(2,1)} async-done(((bf16[16,96,768]{2,0,1:T(8,128)(2,1)}), bf16[16,6,768]{2,0,1:T(8,128)(2,1)}) %reduce-scatter.3.cloned.1.call-update) | async-done | bytes 147472 | tf_op jit(solution)/shard_map/reduce_scatter | solution.py:163
  (236 shorter events, 239.8 us)
Async XLA Ops:
  7.2 2.0 copy-start
  7.2 6.0 copy-start.9
  7.2 55.5 %all-gather.14.cloned.1.call-start = ((), (), s32[]{:S(2)}) async-start(), calls=%async_computation.6 | async-start | bytes 1327104 | tf_op jit(solution)/shard_map/all_gather | solution.py:101
  10.8 4.2 copy-start.2
  10.8 5.7 copy-start.5
  10.8 5.7 copy-start.6
  11.6 100.9 %all-gather.10.cloned.1.call-start = ((), (), s32[]{:S(2)}) async-start(), calls=%async_computation.4 | async-start | bytes 1327104 | tf_op jit(solution)/shard_map/all_gather | solution.py:102
  12.4 135.0 %all-gather.12.cloned.1.call-start = ((), (), s32[]{:S(2)}) async-start(), calls=%async_computation.5 | async-start | bytes 2506752 | tf_op jit(solution)/shard_map/all_gather | solution.py:106
  13.1 255.6 %all-gather.8.cloned.1.call-start = ((), (), s32[]{:S(2)}) async-start(), calls=%async_computation.3 | async-start | bytes 10616832 | tf_op jit(solution)/shard_map/all_gather | solution.py:100
  19.5 1.1 copy-start.8
  19.5 350.1 %all-gather.6.cloned.1.call-start = ((), (), s32[]{:S(2)}) async-start(), calls=%async_computation.2 | async-start | bytes 20054016 | tf_op jit(solution)/shard_map/all_gather | solution.py:105
  20.1 792.1 %reduce-scatter.5.cloned.1.call-start = ((), (), s32[]{:S(2)}) async-start(), calls=%async_computation.8 | async-start | bytes 417792 | tf_op jit(solution)/shard_map/reduce_scatter | solution.py:166
  152.0 217.6 %copy-start.3 = (bf16[128,256]{1,0:T(8,128)(2,1)S(1)}, bf16[128,256]{1,0:T(8,128)(2,1)}, u32[]{:S(2)}) copy-start(bf16[128,256]{1,0:T(8,128)(2,1)} %param.21) | copy-start | bytes 196612
  618.5 0.7 copy-start.10
  674.3 0.8 copy-start.7
  674.7 1.3 copy-start.4
  674.7 1.3 copy-start.11
  676.0 3.6 copy-start.12
  753.0 124.1 %reduce-scatter.3.cloned.1.call-start = ((), (), s32[]{:S(2)}) async-start(), calls=%async_computation.7 | async-start | bytes 2506752 | tf_op jit(solution)/shard_map/reduce_scatter | solution.py:163
  765.7 113.8 %copy-start.1 = (bf16[768,2304]{1,0:T(8,128)(2,1)S(1)}, bf16[768,2304]{1,0:T(8,128)(2,1)}, u32[]{:S(2)}) copy-start(bf16[768,2304]{1,0:T(8,128)(2,1)} %param.26) | copy-start | bytes 10616836
Sparse Core Ops, SparseCore 0:
  11.8 50.8 all-gather.13
  65.5 46.9 all-gather.9
  114.3 33.0 all-gather.11
  150.1 118.6 all-gather.7
  270.3 99.2 all-gather.5
  753.1 59.0 reduce-scatter.4
  814.8 62.2 reduce-scatter.2
where the time goes:
time: 891 us; the launch traced here: 886 us
  waiting for transfers between devices  428 us (48%)
  other arithmetic  170 us (19%)
  local copies, waits for them, and re-layouts  122 us (14%)
  matrix products  95 us (11%)
  blocking collectives  55.5 us (6%)
  between operations  14.5 us (2%)
    all_gather x1, waiting for transfers between devices, shards(): lax.all_gather(right_own, 'row', axis=0, tiled=True)  117 us
    all_gather x1, waiting for transfers between devices, shards(): lax.all_gather(pair_state, 'col', axis=0, tiled=True)  87.7 us
    dynamic_update_slice x32, other arithmetic, rows_blocks(): normed_groups, left_groups = lax.map(one_group, grouped)  87.3 us
    reduce_scatter x1, waiting for transfers between devices, shards(): lax.psum_scatter(summed.astype(jnp.bfloat16), 'col', scatter_dimension=1,...  60.8 us
    dot_general x17, matrix products, gated_branch(): jnp.einsum('ikc,ce->ike', normed, weight, preferred_element_type=jnp.floa...  57.6 us
    pmax x1, blocking collectives, shards(): lax.pmax(local_max.astype(jnp.bfloat16), 'col').astype(local_max.dtype)  55.5 us
    reduce_scatter x1, waiting for transfers between devices, shards(): lax.psum_scatter(totals.astype(jnp.bfloat16), 'col', scatter_dimension=2,...  44.7 us
    all_gather x1, waiting for transfers between devices, shards(): lax.all_gather(values_own, 'row', axis=1, tiled=True)  44.2 us
  transfers between devices with their start and end apart: 7, of which 7 were waited for; matrix products, arithmetic and copies ran while one was open for 6% of the time, Pallas kernels for 0%

commit v1 on v0

--- a/solution.py
+++ b/solution.py
@@ -97,7 +97,9 @@
     own_mask = valid_own[:, None] * valid_all[None, :]
     right_own = gated_branch(normed_own, right_weight, own_mask)
     right_cols, keys_cols, values_cols = (
-        lax.all_gather(right_own, "row", axis=0, tiled=True),
+        jnp.concatenate(
+            lax.all_to_all(jnp.stack([right_own] * lax.axis_size("row")), "row", 0, 0), axis=0
+        ),
         lax.all_gather(keys_own, "row", axis=1, tiled=True),
         lax.all_gather(values_own, "row", axis=1, tiled=True),
     )

time: 891 us -> 851 us (0.955)
  waiting for transfers between devices: 428 us -> 376 us
    all_gather x1 -> x0, waiting for transfers between devices: 117 us -> none  [shards(): lax.all_gather(right_own, 'row', axis=0, tiled=True)]
    all_gather x1, waiting for transfers between devices: 44.2 us -> 89.4 us  [shards(): lax.all_gather(values_own, 'row', axis=1, tiled=True)]
    all_gather x1, waiting for transfers between devices: 41.2 us -> 63.6 us  [shards(): lax.all_gather(keys_own, 'row', axis=1, tiled=True)]
    all_gather x1 -> x0, local copies, waits for them, and re-layouts: 13.2 us -> none  [shards(): lax.all_gather(right_own, 'row', axis=0, tiled=True)]
    reshape x0 -> x1, local copies, waits for them, and re-layouts: none -> 13.1 us  [shards(): jnp.concatenate(lax.all_to_all(jnp.stack([right_own] * lax.axis_size('row...]
  transfers between devices with their start and end apart: 7 -> 7, of which waited for: 7 -> 6; matrix products, arithmetic and copies ran while one was open for 6% -> 7% of each run, Pallas kernels for 0% -> 0%
where the time goes in v1:
time: 851 us; the launch traced here: 846 us
  waiting for transfers between devices  376 us (44%)
  other arithmetic  168 us (20%)
  local copies, waits for them, and re-layouts  128 us (15%)
  matrix products  94.9 us (11%)
  blocking collectives  55.5 us (7%)
  between operations  14.5 us (2%)
    all_gather x1, waiting for transfers between devices, shards(): lax.all_gather(values_own, 'row', axis=1, tiled=True)  89.4 us
    dynamic_update_slice x32, other arithmetic, rows_blocks(): normed_groups, left_groups = lax.map(one_group, grouped)  87.3 us
    all_gather x1, waiting for transfers between devices, shards(): lax.all_gather(pair_state, 'col', axis=0, tiled=True)  85.5 us
    all_gather x1, waiting for transfers between devices, shards(): lax.all_gather(keys_own, 'row', axis=1, tiled=True)  63.6 us
    reduce_scatter x1, waiting for transfers between devices, shards(): lax.psum_scatter(summed.astype(jnp.bfloat16), 'col', scatter_dimension=1,...  60.7 us
    dot_general x17, matrix products, gated_branch(): jnp.einsum('ikc,ce->ike', normed, weight, preferred_element_type=jnp.floa...  57.6 us
    pmax x1, blocking collectives, shards(): lax.pmax(local_max.astype(jnp.bfloat16), 'col').astype(local_max.dtype)  55.5 us
    reduce_scatter x1, waiting for transfers between devices, shards(): lax.psum_scatter(totals.astype(jnp.bfloat16), 'col', scatter_dimension=2,...  44.8 us
  transfers between devices with their start and end apart: 7, of which 6 were waited for; matrix products, arithmetic and copies ran while one was open for 7% of the time, Pallas kernels for 0%

profile of v1, /device:TPU:0, one launch (start us, length us, event | category | flops | bytes accessed | tf_op | source)
XLA Modules:
  0.0 846.3 jit_solution(4060723777575588398)
XLA Ops:
  18.0 5.9 stack.2
  23.9 7.8 all-to-all-start
  33.0 63.6 %all-gather.11.cloned.1.call-done = bf16[16,48,768]{2,0,1:T(8,128)(2,1)} async-done(((bf16[16,6,768]{2,0,1:T(8,128)(2,1)}), bf16[16,48,768]{2,0,1:T(8,128)(2,1)}) %all-gather.11.cloned.1.call-update) | async-done | bytes 1179664 | tf_op jit(solution)/shard_map/all_gather | solution.py:103
  96.6 5.7 reshape.296
  102.3 89.4 %all-gather.7.cloned.1.call-done = bf16[16,48,768]{2,0,1:T(8,128)(2,1)} async-done(((bf16[16,6,768]{2,0,1:T(8,128)(2,1)}), bf16[16,48,768]{2,0,1:T(8,128)(2,1)}) %all-gather.7.cloned.1.call-update) | async-done | bytes 1179664 | tf_op jit(solution)/shard_map/all_gather | solution.py:104
  191.7 4.3 copy.104
  196.0 30.6 %all-gather.9.cloned.1.call-done = bf16[16,96,768]{2,0,1:T(8,128)(2,1)} async-done(((bf16[16,6,768]{2,0,1:T(8,128)(2,1)}), bf16[16,96,768]{2,0,1:T(8,128)(2,1)}) %all-gather.9.cloned.1.call-update) | async-done | bytes 2359312 | tf_op jit(solution)/shard_map/all_gather | solution.py:108
  226.5 4.6 copy.105
  231.1 13.1 %copy.99 = bf16[48,768,128]{1,0,2:T(8,128)(2,1)} copy(bf16[48,768,128]{2,1,0:T(8,128)(2,1)} %bitcast.10) | data formatting | bytes 18874368 | tf_op jit(solution)/shard_map/reshape | solution.py:100
  244.2 85.5 %all-gather.5.cloned.1.call-done = bf16[96,768,128]{2,1,0:T(8,128)(2,1)} async-done(((bf16[6,768,128]{2,1,0:T(8,128)(2,1)}), bf16[96,768,128]{2,1,0:T(8,128)(2,1)}) %all-gather.5.cloned.1.call-update) | async-done | bytes 18874384 | tf_op jit(solution)/shard_map/all_gather | solution.py:107
  329.7 212.1 %while.12 = (s32[]{:T(128)}, bf16[16,6,768,128]{3,2,1,0:T(8,128)(2,1)}, bf16[16,6,768,128]{3,2,1,0:T(8,128)(2,1)}, bf16[16,6,768,128]{3,2,1,0:T(8,128)(2,1)}, f3...) while((s32[]{:T(128)}, ...), condition=%wide.region_3.4_spmd, body=%wide.region_0.0_spmd.sunk | while | flops 314975232 | bytes 16826032 | solution.py:44
  339.2 3.9 fusion.82
  378.9 3.9 fusion.82
  541.8 24.4 %copy.100 = bf16[96,768,128]{1,0,2:T(8,128)(2,1)} copy(bf16[96,768,128]{2,1,0:T(8,128)(2,1)} %bitcast.98) | data formatting | bytes 37748736 | tf_op jit(solution)/shard_map/reshape | solution.py:47
  566.2 12.4 %bitcast_reduce_fusion = (f32[96,48]{0,1:T(8,128)S(1)}, f32[128,48,96]{2,1,0:T(8,128)S(1)}) fusion(bf16[48,768,128]{1,0,2:T(8,128)(2,1)} %copy.99, bf16[96,768,128]{1,0,2:T(8,128)(2,1)} %copy.100), kind=kOutput, calls=%fused_computation.42 | convolution fusion | flops 906554880 | bytes 30689280 | tf_op jit(solution)/shard_map/ikc,jkc->ijc/dot_general | solution.py:125
  584.1 31.1 %reshape_reshape.3 = bf16[96,8,16,6,128]{4,3,2,1,0:T(8,128)(2,1)} reshape(bf16[16,6,768,128]{3,2,1,0:T(8,128)(2,1)} %get-tuple-element.45) | data formatting | bytes 37748736 | tf_op jit(solution)/shard_map/reshape;reshape | solution.py:120
  617.6 16.7 %copy.96 = bf16[96,768,128]{2,0,1:T(8,128)(2,1)S(1)} copy(bf16[96,768,128]{2,1,0:T(8,128)(2,1)} %bitcast.96) | data formatting | bytes 37748736 | tf_op jit(solution)/shard_map/all_gather | solution.py:107
  642.5 9.0 %select_reduce_fusion = (bf16[16,16,96]{2,1,0:T(8,128)(2,1)S(1)}, f32[16,16,96,48]{2,3,1,0:T(8,128)}) fusion(f32[16,96,48]{1,2,0:T(8,128)S(1)} %copy.112, pred[96,48]{0,1:T(8,128)(4,1)S(1)} %compare_or_fusion, bf16[16,96,16,48]{1,3,2,0:T(8,128)(2,1)} %bitcast.102, bf16[16,48,16,48]{3,2,0,1:T(8,128)(2,1)} %reshape.296), kind=kOutput, calls=%fused_computation.34 | convolution fusion | flops 117940224 | bytes 8606208 | tf_op jit(solution)/shard_map/sihd,sjhd->shij/dot_general | solution.py:143
  651.4 55.5 %pmax.7 = bf16[16,16,96]{2,1,0:T(8,128)(2,1)S(1)} all-reduce(bf16[16,16,96]{2,1,0:T(8,128)(2,1)S(1)} %get-tuple-element.90), channel_id=1, replica_groups=mesh['row'=8,'col'=16] {'col'}, use_global_device_ids=true, to_apply=%region_11.12 | all-reduce | flops 24576 | bytes 98304 | tf_op jit(solution)/shard_map/pmax | solution.py:156
  707.0 5.0 fusion.65
  713.3 7.2 convolution_convert_fusion
  720.5 4.9 copy.113
  727.5 44.8 %reduce-scatter.5.cloned.1.call-done = bf16[16,16,6]{1,0,2:T(8,128)(2,1)} async-done(((bf16[16,16,96]{1,0,2:T(8,128)(2,1)}), bf16[16,16,6]{1,0,2:T(8,128)(2,1)}) %reduce-scatter.5.cloned.1.call-update) | async-done | bytes 3088 | tf_op jit(solution)/shard_map/reduce_scatter | solution.py:168
  776.3 60.7 %reduce-scatter.3.cloned.1.call-done = bf16[16,6,768]{2,0,1:T(8,128)(2,1)} async-done(((bf16[16,96,768]{2,0,1:T(8,128)(2,1)}), bf16[16,6,768]{2,0,1:T(8,128)(2,1)}) %reduce-scatter.3.cloned.1.call-update) | async-done | bytes 147472 | tf_op jit(solution)/shard_map/reduce_scatter | solution.py:165
  (236 shorter events, 241.5 us)
Async XLA Ops:
  7.2 2.0 copy-start
  7.2 89.4 %all-gather.11.cloned.1.call-start = ((), (), s32[]{:S(2)}) async-start(), calls=%async_computation.6 | async-start | bytes 1327104 | tf_op jit(solution)/shard_map/all_gather | solution.py:103
  10.8 2.9 copy-start.9
  10.8 3.0 copy-start.2
  10.8 4.9 copy-start.5
  10.8 4.9 copy-start.6
  11.7 180.0 %all-gather.7.cloned.1.call-start = ((), (), s32[]{:S(2)}) async-start(), calls=%async_computation.4 | async-start | bytes 1327104 | tf_op jit(solution)/shard_map/all_gather | solution.py:104
  12.4 214.1 %all-gather.9.cloned.1.call-start = ((), (), s32[]{:S(2)}) async-start(), calls=%async_computation.5 | async-start | bytes 2506752 | tf_op jit(solution)/shard_map/all_gather | solution.py:108
  13.1 316.6 %all-gather.5.cloned.1.call-start = ((), (), s32[]{:S(2)}) async-start(), calls=%async_computation.3 | async-start | bytes 20054016 | tf_op jit(solution)/shard_map/all_gather | solution.py:107
  23.9 8.3 copy-start.8
  23.9 207.3 %all-to-all-start = ((bf16[8,6,768,128]{3,2,1,0:T(8,128)(2,1)}), bf16[8,6,768,128]{3,2,1,0:T(8,128)(2,1)}, u32[]{:S(2)}, u32[]{:S(2)}) async-start(bf16[8,6,768,128]{3,2,1,0:T(8,128)(2,1)} %stack.2), calls=%async_computation | async-start | bytes 18874368 | tf_op jit(solution)/shard_map/all_to_all | solution.py:101
  31.7 740.6 %reduce-scatter.5.cloned.1.call-start = ((), (), s32[]{:S(2)}) async-start(), calls=%async_computation.8 | async-start | bytes 417792 | tf_op jit(solution)/shard_map/reduce_scatter | solution.py:168
  231.1 98.6 %copy-start.3 = (bf16[128,256]{1,0:T(8,128)(2,1)S(1)}, bf16[128,256]{1,0:T(8,128)(2,1)}, u32[]{:S(2)}) copy-start(bf16[128,256]{1,0:T(8,128)(2,1)} %param.21) | copy-start | bytes 196612
  578.6 0.7 copy-start.10
  634.4 0.8 copy-start.7
  634.8 1.3 copy-start.4
  634.8 1.3 copy-start.11
  636.1 3.6 copy-start.12
  713.0 124.0 %reduce-scatter.3.cloned.1.call-start = ((), (), s32[]{:S(2)}) async-start(), calls=%async_computation.7 | async-start | bytes 2506752 | tf_op jit(solution)/shard_map/reduce_scatter | solution.py:165
  725.7 113.7 %copy-start.1 = (bf16[768,2304]{1,0:T(8,128)(2,1)S(1)}, bf16[768,2304]{1,0:T(8,128)(2,1)}, u32[]{:S(2)}) copy-start(bf16[768,2304]{1,0:T(8,128)(2,1)} %param.26) | copy-start | bytes 10616836
Sparse Core Ops, SparseCore 0:
  11.8 84.7 all-gather.10
  99.5 92.1 all-gather.6
  193.4 33.0 all-gather.8
  228.1 101.5 all-gather.4
  713.2 59.0 reduce-scatter.4
  774.7 62.3 reduce-scatter.2
